TPU v7x, 32 devices: a whole 2x2x4 slice. The times are simulated.
32 devices in a mesh: lat: 8 (over z, x), ch: 4 (over y, core).
Axes of the slice: x: 2, y: 2, z: 4, core: 2. Of those that a mesh axis runs over, the one named last changes fastest.
Arguments:
- tokens: bfloat16 [1, 16, 8, 69120], P(None, 'lat', 'ch'), may hold values from -6 to 6
- cotangent: bfloat16 [1, 16, 8, 69120], P(None, 'lat', 'ch'), may hold values from -6 to 6
- first_weight: bfloat16 [2, 8, 96, 96], P(None, 'ch'), may hold values from -0.4375 to 0.4375
- first_bias: bfloat16 [2, 8, 96], P(None, 'ch'), may hold values from -6 to 6
- second_weight: bfloat16 [2, 8, 96, 96], P(None, 'ch'), may hold values from -0.4375 to 0.4375
- relu_mask: int32 [1, 2, 8, 256, 1536], P(None, None, 'ch', 'lat'), may hold values 0 or 1
- shrink_mask: int32 [1, 2, 8, 256, 1536], P(None, None, 'ch', 'lat'), may hold values 0 or 1
Outputs:
- token_gradient: bfloat16 [1, 16, 8, 69120], P(None, 'lat', 'ch')
- first_gradient: float32 [2, 8, 96, 96], P(None, 'ch')
- bias_gradient: float32 [2, 8, 96], P(None, 'ch')
- second_gradient: float32 [2, 8, 96, 96], P(None, 'ch')
All inputs are finite; a program needn't handle non-finite values. No bound on the sum of `relu_mask` or of `shrink_mask` on one device may be relied on, other than what follows from the above.
Results may differ from a plain program's by a relative error of at most 0.0093.
Values may be sent and summed in bfloat16 or wider, within the bound.
No kernel may reach another device: no remote copies, remote signals or barrier semaphores. Data moves between devices by JAX's collectives and lax.ppermute only.
A program may use at most 64 MiB of HBM per device.

v0:
```python
import math

import jax
import jax.numpy as jnp
from jax import lax
from jax.sharding import PartitionSpec as P

WAVES = 256


def east_basis(count, waves):
    column = jnp.arange(count, dtype=jnp.int32)[:, None]
    number = jnp.arange(waves, dtype=jnp.int32)[None, :]
    phase = (column * number % count).astype(jnp.float32) * (2.0 * math.pi / count)
    factor = 1.0 / math.sqrt(count)
    return jnp.stack([jnp.cos(phase) * factor, -jnp.sin(phase) * factor], axis=1)


def north_basis(count):
    column = jnp.arange(count, dtype=jnp.int32)[:, None]
    number = jnp.arange(count, dtype=jnp.int32)[None, :]
    phase = (column * number % count).astype(jnp.float32) * (2.0 * math.pi / count)
    factor = 1.0 / math.sqrt(count)
    cosine = jnp.cos(phase) * factor
    sine = jnp.sin(phase) * factor
    upper = jnp.concatenate([cosine, sine], axis=1)
    lower = jnp.concatenate([-sine, cosine], axis=1)
    return jnp.concatenate([upper, lower], axis=0)


def complex_mix(left_real, left_imag, right_real, right_imag, form):
    real_part = jnp.einsum(
        form, left_real, right_real, preferred_element_type=jnp.float32
    ) - jnp.einsum(form, left_imag, right_imag, preferred_element_type=jnp.float32)
    imag_part = jnp.einsum(
        form, left_real, right_imag, preferred_element_type=jnp.float32
    ) + jnp.einsum(form, left_imag, right_real, preferred_element_type=jnp.float32)
    return (real_part, imag_part)


def local(tokens, cotangent, first_weight, first_bias, second_weight, relu_mask, shrink_mask):
    batches, lat_rows, blocks_dev, flat_east = tokens.shape
    block_width = first_weight.shape[2]
    east_cells = flat_east // block_width
    east_table = east_basis(east_cells, WAVES).astype(jnp.bfloat16)

    def to_waves(field):
        grid = field.reshape(batches, lat_rows, blocks_dev, east_cells, block_width)
        return jnp.einsum(
            "bhnwe,wsk->bsnkhe", grid, east_table, preferred_element_type=jnp.float32
        ).astype(jnp.bfloat16)

    spec_tokens = lax.all_to_all(to_waves(tokens), "lat", split_axis=3, concat_axis=4, tiled=True)
    spec_cotangent = lax.all_to_all(
        to_waves(cotangent), "lat", split_axis=3, concat_axis=4, tiled=True
    )
    wave_dev = spec_tokens.shape[3]
    north_cells = spec_tokens.shape[4]
    north_table = (
        north_basis(north_cells).astype(jnp.bfloat16).reshape(2, north_cells, 2, north_cells)
    )
    factor = 1.0 / math.sqrt(north_cells * WAVES)
    shape_modes = (batches, 2, blocks_dev, wave_dev, north_cells, block_width)

    def to_modes(spec):
        return jnp.einsum(
            "tqsp,bsnkpe->btnkqe", north_table, spec, preferred_element_type=jnp.float32
        ).astype(jnp.bfloat16)

    relu_keep = relu_mask.reshape(shape_modes).astype(jnp.float32)
    shrink_keep = shrink_mask.reshape(shape_modes).astype(jnp.bfloat16)
    modes = to_modes(spec_tokens)
    upstream = to_modes(spec_cotangent) * shrink_keep
    before_real, before_imag = complex_mix(
        modes[:, 0], modes[:, 1], first_weight[0], first_weight[1], "bnkqe,nef->bnkqf"
    )
    bias_real = first_bias[0].astype(jnp.float32)[None, :, None, None, :]
    bias_imag = first_bias[1].astype(jnp.float32)[None, :, None, None, :]
    hidden_real = (relu_keep[:, 0] * (before_real + bias_real)).astype(jnp.bfloat16)
    hidden_imag = (relu_keep[:, 1] * (before_imag + bias_imag)).astype(jnp.bfloat16)
    second_real, second_imag = complex_mix(
        hidden_real, -hidden_imag, upstream[:, 0], upstream[:, 1], "bnkqe,bnkqf->nef"
    )
    second_grad = jnp.stack([second_real, second_imag]) * factor
    back_real, back_imag = complex_mix(
        upstream[:, 0], upstream[:, 1], second_weight[0], -second_weight[1], "bnkqf,nef->bnkqe"
    )
    inner_real = (relu_keep[:, 0] * back_real).astype(jnp.bfloat16)
    inner_imag = (relu_keep[:, 1] * back_imag).astype(jnp.bfloat16)
    first_real, first_imag = complex_mix(
        modes[:, 0], -modes[:, 1], inner_real, inner_imag, "bnkqe,bnkqf->nef"
    )
    first_grad = jnp.stack([first_real, first_imag]) * factor
    bias_grad = (
        jnp.stack(
            [
                jnp.sum(inner_real.astype(jnp.float32), axis=(0, 2, 3)),
                jnp.sum(inner_imag.astype(jnp.float32), axis=(0, 2, 3)),
            ]
        )
        * factor
    )
    first_grad, bias_grad, second_grad = lax.psum((first_grad, bias_grad, second_grad), "lat")
    mode_real, mode_imag = complex_mix(
        inner_real, inner_imag, first_weight[0], -first_weight[1], "bnkqf,nef->bnkqe"
    )
    stacked = jnp.stack([mode_real, mode_imag], axis=1).astype(jnp.bfloat16)
    returned = jnp.einsum(
        "tqsp,btnkqe->bsnkpe", north_table, stacked, preferred_element_type=jnp.float32
    ).astype(jnp.bfloat16)
    returned = lax.all_to_all(returned, "lat", split_axis=4, concat_axis=3, tiled=True)
    token_grad = jnp.einsum(
        "bsnkhe,wsk->bhnwe", returned, east_table, preferred_element_type=jnp.float32
    )
    token_grad = token_grad.reshape(batches, lat_rows, blocks_dev, flat_east)
    token_gradient = (token_grad + cotangent.astype(jnp.float32)).astype(jnp.bfloat16)
    return (token_gradient, first_grad, bias_grad, second_grad)


def solution(mesh):
    return jax.shard_map(
        local,
        mesh=mesh,
        in_specs=(
            P(None, "lat", "ch", None),
            P(None, "lat", "ch", None),
            P(None, "ch", None, None),
            P(None, "ch", None),
            P(None, "ch", None, None),
            P(None, None, "ch", "lat", None),
            P(None, None, "ch", "lat", None),
        ),
        out_specs=(
            P(None, "lat", "ch", None),
            P(None, "ch", None, None),
            P(None, "ch", None),
            P(None, "ch", None, None),
        ),
        check_vma=False,
    )
```

profile of v0, /device:TPU:0, one launch (start us, length us, event | category | flops | bytes accessed | tf_op | source)
XLA Modules:
  0.0 157.0 jit_solution(12354883418392423553)
XLA Ops:
  7.2 3.3 %multiply_convert_fusion = (bf16[720,1,256]{2,0,1:T(8,128)(2,1)S(1)}, bf16[720,1,256]{2,0,1:T(8,128)(2,1)S(1)}) fusion(), kind=kLoop, calls=%fused_computation.70 | loop fusion | flops 2580480 | bytes 737280 | tf_op jit(solution)/shard_map/convert.17
  10.5 2.0 %reshape.257 = bf16[2,2,720,96]{3,2,1,0:T(8,128)(2,1)S(1)} reshape(bf16[1,2,2,69120]{3,2,1,0:T(2,128)(2,1)} %param.7) | data formatting | bytes 1105920 | tf_op jit(solution)/shard_map/reshape.34
  13.0 1.2 copy.86
  14.2 7.3 %all-to-all-start.2 = ((bf16[1,2,2,256,2,96]{5,2,4,1,0,3:T(2,128)(2,1)}), bf16[1,2,2,256,2,96]{5,2,4,1,0,3:T(2,128)(2,1)}, u32[]{:S(2)}, u32[]{:S(2)}) async-start(bf16[1,2,2,256,2,96]{5,2,4,1,0,3:T(2,128)(2,1)} %copy.86), calls=%async_computation.2 | async-start | bytes 1048576 | tf_op jit(solution)/shard_map/all_to_all | solution.py:53
  23.5 1.3 fusion.25
  24.8 2.0 %copy.69 = bf16[1,2,2,256,2,96]{5,2,4,1,0,3:T(2,128)(2,1)} copy(bf16[1,2,2,256,2,96]{3,5,2,4,1,0:T(8,128)(2,1)} %fusion.25) | data formatting | bytes 786432 | tf_op jit(solution)/shard_map/convert_element_type | solution.py:51
  26.8 1.2 convert_element_type.163
  29.6 6.4 %all-to-all-done.2 = bf16[1,2,2,256,2,96]{5,2,4,1,0,3:T(2,128)(2,1)} async-done(((bf16[1,2,2,256,2,96]{5,2,4,1,0,3:T(2,128)(2,1)}), bf16[1,2,2,256,2,96]{5,2,4,1,0,3:T(2,128)(2,1)}, u32[]{:S(2)}, u32[]{:S(2)}) %all-to-all-start.2) | async-done | bytes 393248 | tf_op jit(solution)/shard_map/all_to_all | solution.py:53
  36.0 3.6 %all-to-all-start = ((bf16[1,2,2,256,2,96]{5,2,4,1,0,3:T(2,128)(2,1)}), bf16[1,2,2,256,2,96]{5,2,4,1,0,3:T(2,128)(2,1)S(1)}, u32[]{:S(2)}, u32[]{:S(2)}) async-start(bf16[1,2,2,256,2,96]{5,2,4,1,0,3:T(2,128)(2,1)} %copy.69), calls=%async_computation | async-start | bytes 1048576 | tf_op jit(solution)/shard_map/all_to_all | solution.py:54
  39.7 1.1 copy.87
  41.7 1.0 fusion.53
  42.8 1.0 fusion.55
  43.8 10.5 %all-to-all-done = bf16[1,2,2,256,2,96]{5,2,4,1,0,3:T(2,128)(2,1)S(1)} async-done(((bf16[1,2,2,256,2,96]{5,2,4,1,0,3:T(2,128)(2,1)}), bf16[1,2,2,256,2,96]{5,2,4,1,0,3:T(2,128)(2,1)S(1)}, u32[]{:S(2)}, u32[]{:S(2)}) %all-to-all-start) | async-done | bytes 393248 | tf_op jit(solution)/shard_map/all_to_all | solution.py:54
  58.5 0.9 convert_reduce_fusion.1
  59.9 1.0 convert_reduce_fusion
  63.6 1.3 copy.81
  65.0 3.7 %all-to-all-start.1 = ((bf16[1,2,2,32,16,96]{5,1,3,2,0,4:T(2,128)(2,1)}), bf16[1,2,2,32,16,96]{5,1,3,2,0,4:T(2,128)(2,1)S(1)}, u32[]{:S(2)}, u32[]{:S(2)}) async-start(bf16[1,2,2,32,16,96]{5,1,3,2,0,4:T(2,128)(2,1)} %copy.81), calls=%async_computation.1 | async-start | bytes 1048576 | tf_op jit(solution)/shard_map/all_to_all | solution.py:111
  68.7 1.4 fusion.29
  72.7 22.6 %psum.22 = f32[2,2,96]{2,1,0:T(2,128)} all-reduce(f32[2,2,96]{2,1,0:T(2,128)S(1)} %maximum_multiply_fusion.2), channel_id=1, replica_groups=mesh['lat'=8,'ch'=4] {'lat'}, use_global_device_ids=true, to_apply=%region_3.4 | all-reduce | flops 384 | bytes 3072 | tf_op jit(solution)/shard_map/psum | solution.py:103
  96.5 1.5 reshape.256
  97.9 1.4 add_convert_fusion
  99.3 47.6 %all-reduce.3.cloned.1.call-done = (f32[2,2,96,96]{3,2,1,0:T(8,128)}, f32[2,2,96,96]{3,2,1,0:T(8,128)}) async-done(((f32[2,2,96,96]{3,2,1,0:T(8,128)}, f32[2,2,96,96]{3,2,1,0:T(8,128)}), (f32[2,2,96,96]{3,2,1,0:T(8,128)}, f32[2,2,96,96]{3,2,1,0:T(8,128)})) %all-reduce.3.cloned.1.call-update) | async-done | bytes 294928 | tf_op jit(solution)/shard_map/psum | solution.py:103
  146.9 1.6 %copy.200 = f32[2,2,96,96]{3,2,1,0:T(8,128)} copy(f32[2,2,96,96]{3,2,1,0:T(8,128)} %get-tuple-element.23) | data formatting | bytes 294912
  148.5 1.6 %copy.201 = f32[2,2,96,96]{3,2,1,0:T(8,128)} copy(f32[2,2,96,96]{3,2,1,0:T(8,128)} %get-tuple-element.25) | data formatting | bytes 294912
  (79 shorter events, 16.0 us)
Async XLA Ops:
  10.5 13.1 %copy-start.3 = (bf16[720,1,256]{2,0,1:T(8,128)(2,1)}, bf16[720,1,256]{2,0,1:T(8,128)(2,1)S(1)}, u32[]{:S(2)}) copy-start(bf16[720,1,256]{2,0,1:T(8,128)(2,1)S(1)} %get-tuple-element.18) | copy-start | bytes 1105924
  10.5 13.1 %copy-start.5 = (bf16[720,1,256]{2,0,1:T(8,128)(2,1)}, bf16[720,1,256]{2,0,1:T(8,128)(2,1)S(1)}, u32[]{:S(2)}) copy-start(bf16[720,1,256]{2,0,1:T(8,128)(2,1)S(1)} %get-tuple-element.19) | copy-start | bytes 1105924
  13.0 8.8 %copy-start.7 = (s32[1,2,2,32,1536]{4,3,2,1,0:T(8,128)S(1)}, s32[1,2,2,32,1536]{4,3,2,1,0:T(8,128)}, u32[]{:S(2)}) copy-start(s32[1,2,2,32,1536]{4,3,2,1,0:T(8,128)} %param.12) | copy-start | bytes 2359300
  14.2 21.9 %all-to-all-start.2 = ((bf16[1,2,2,256,2,96]{5,2,4,1,0,3:T(2,128)(2,1)}), bf16[1,2,2,256,2,96]{5,2,4,1,0,3:T(2,128)(2,1)}, u32[]{:S(2)}, u32[]{:S(2)}) async-start(bf16[1,2,2,256,2,96]{5,2,4,1,0,3:T(2,128)(2,1)} %copy.86), calls=%async_computation.2 | async-start | bytes 1048576 | tf_op jit(solution)/shard_map/all_to_all | solution.py:53
  21.7 1.1 copy-start
  26.8 2.1 %copy-start.12 = (bf16[2,2,96]{2,1,0:T(2,128)(2,1)S(1)}, bf16[2,2,96]{2,1,0:T(2,128)(2,1)}, u32[]{:S(2)}) copy-start(bf16[2,2,96]{2,1,0:T(2,128)(2,1)} %param.10) | copy-start | bytes 2308
  36.0 18.3 %all-to-all-start = ((bf16[1,2,2,256,2,96]{5,2,4,1,0,3:T(2,128)(2,1)}), bf16[1,2,2,256,2,96]{5,2,4,1,0,3:T(2,128)(2,1)S(1)}, u32[]{:S(2)}, u32[]{:S(2)}) async-start(bf16[1,2,2,256,2,96]{5,2,4,1,0,3:T(2,128)(2,1)} %copy.69), calls=%async_computation | async-start | bytes 1048576 | tf_op jit(solution)/shard_map/all_to_all | solution.py:54
  40.8 1.0 copy-start.2
  55.0 0.9 copy-start.8
  55.3 1.1 copy-start.1
  55.3 1.0 copy-start.9
  65.0 30.4 %all-to-all-start.1 = ((bf16[1,2,2,32,16,96]{5,1,3,2,0,4:T(2,128)(2,1)}), bf16[1,2,2,32,16,96]{5,1,3,2,0,4:T(2,128)(2,1)S(1)}, u32[]{:S(2)}, u32[]{:S(2)}) async-start(bf16[1,2,2,32,16,96]{5,1,3,2,0,4:T(2,128)(2,1)} %copy.81), calls=%async_computation.1 | async-start | bytes 1048576 | tf_op jit(solution)/shard_map/all_to_all | solution.py:111
  68.6 78.3 %all-reduce.3.cloned.1.call-start = ((), (), s32[]{:S(2)}) async-start(), calls=%async_computation.3 | async-start | bytes 786432 | tf_op jit(solution)/shard_map/psum | solution.py:103
  68.7 1.4 copy-start.14
  68.7 1.7 %copy-start.13 = (f32[2,96,96]{2,1,0:T(8,128)S(1)}, f32[2,96,96]{2,1,0:T(8,128)}, u32[]{:S(2)}) copy-start(f32[2,96,96]{2,1,0:T(8,128)} %convolution_bitcast_fusion.4) | copy-start | bytes 221188
  68.7 2.7 %copy-start.16 = (f32[2,96,96]{2,1,0:T(8,128)S(1)}, f32[2,96,96]{2,1,0:T(8,128)}, u32[]{:S(2)}) copy-start(f32[2,96,96]{2,1,0:T(8,128)} %convolution_bitcast_fusion.10) | copy-start | bytes 221188
  70.4 1.2 copy-start.15
  71.7 1.0 copy-start.10
  71.7 1.0 copy-start.11
  71.7 23.8 %copy-start.4 = (bf16[720,1,256]{2,0,1:T(8,128)(2,1)S(1)}, bf16[720,1,256]{2,0,1:T(8,128)(2,1)}, u32[]{:S(2)}) copy-start(bf16[720,1,256]{2,0,1:T(8,128)(2,1)} %copy-done.3) | copy-start | bytes 1105924
  71.7 23.8 %copy-start.6 = (bf16[720,1,256]{2,0,1:T(8,128)(2,1)S(1)}, bf16[720,1,256]{2,0,1:T(8,128)(2,1)}, u32[]{:S(2)}) copy-start(bf16[720,1,256]{2,0,1:T(8,128)(2,1)} %copy-done.5) | copy-start | bytes 1105924
Sparse Core Ops, SparseCore 0:
  73.4 73.4 all-reduce.2
where the time goes:
time: 158 us; the launch traced here: 157 us
  waiting for transfers between devices  64.6 us (41%)
  blocking collectives  22.6 us (14%)
  local copies, waits for them, and re-layouts  17.4 us (11%)
  matrix products  15 us (9%)
  starting transfers between devices  14.6 us (9%)
  between operations  14.5 us (9%)
  other arithmetic  8.23 us (5%)
    psum x1, waiting for transfers between devices, local(): lax.psum((first_grad, bias_grad, second_grad), 'lat')  47.6 us
    psum x1, blocking collectives, local(): lax.psum((first_grad, bias_grad, second_grad), 'lat')  22.6 us
    all_to_all x1, waiting for transfers between devices, local(): lax.all_to_all(to_waves(cotangent), 'lat', split_axis=3, concat_axis=4, t...  10.5 us
    all_to_all x1, starting transfers between devices, local(): lax.all_to_all(to_waves(tokens), 'lat', split_axis=3, concat_axis=4, tile...  7.28 us
    all_to_all x1, waiting for transfers between devices, local(): lax.all_to_all(to_waves(tokens), 'lat', split_axis=3, concat_axis=4, tile...  6.44 us
    unnamed x36, local copies, waits for them, and re-layouts  4.46 us
    dot_general x5, matrix products, complex_mix(): jnp.einsum(form, left_imag, right_imag, preferred_element_type=jnp.float32)  4.39 us
    all_to_all x1, starting transfers between devices, local(): lax.all_to_all(returned, 'lat', split_axis=4, concat_axis=3, tiled=True)  3.65 us
  transfers between devices with their start and end apart: 4, of which 3 were waited for; matrix products, arithmetic and copies ran while one was open for 12% of the time, Pallas kernels for 0%

commit v1 on v0

v1 whole, which is shorter than its diff:
```python
import functools
import math

import jax
import jax.numpy as jnp
import numpy as np
from jax import lax
from jax.experimental import pallas as pl
from jax.experimental.pallas import tpu as pltpu
from jax.sharding import PartitionSpec as P

WAVES = 256
BF16 = jnp.bfloat16
F32 = jnp.float32


def group_of(wave_dev):
    return 16 if wave_dev % 16 == 0 else wave_dev


def east_rows(count, waves, owners):
    wave_dev = waves // owners
    group = group_of(wave_dev)
    phase = np.outer(np.arange(waves), np.arange(count)) % count * (2.0 * math.pi / count)
    table = np.stack([np.cos(phase), -np.sin(phase)]) / math.sqrt(count)
    table = table.reshape(2, owners, wave_dev // group, group, count)
    return table.transpose(1, 2, 0, 3, 4).reshape(2 * waves, count)


def north_rows(owners, rows, group):
    cells = owners * rows
    phase = np.outer(np.arange(cells), np.arange(cells)) % cells * (2.0 * math.pi / cells)
    cosine, sine = np.cos(phase) / math.sqrt(cells), np.sin(phase) / math.sqrt(cells)
    table = np.stack([np.stack([cosine, sine], 1), np.stack([-sine, cosine], 1)])
    table = table.reshape(2, cells, 2, owners, rows)
    full = np.einsum("tqsjr,kl->rtkqjsl", table, np.eye(group))
    return full.reshape(rows, 2 * group * cells, owners * 2 * group)


def dot(left, right, form=((1,), (0,))):
    return lax.dot_general(left, right, (form, ((), ())), preferred_element_type=F32)


ROWS, COLS = ((0,), (0,)), ((1,), (1,))


def mix_kernel(geo, spec_ref, table_ref, back_ref, weight_ref, bias_ref, relu_ref, shrink_ref,
               back_out, *rest):
    *grad_outs, first_sum, second_sum, bias_sum = rest
    owners, groups, group, rows, blocks, width, packed = geo
    span = owners * 2 * group
    half = table_ref.shape[1] // 2
    one_real, one_imag, two_real, two_imag = (weight_ref[i] for i in range(4))
    field = rows * width
    for g in range(groups):
        if groups == 1:
            spec = spec_ref[...]
        else:
            spec = spec_ref[...].reshape(owners, groups, 2 * group, 2 * field)
            spec = spec[:, g].reshape(span, 2 * field)

        def modes_of(base):
            total = None
            for r in range(rows):
                term = dot(table_ref[r], spec[:, base + r * width : base + (r + 1) * width])
                total = term if total is None else total + term
            return total.astype(BF16)

        at = slice(g * half, (g + 1) * half)
        modes = modes_of(0)
        spectral = modes_of(field)
        mode_real, mode_imag = modes[:half], modes[half:]
        relu_real = relu_ref[0, at, :].astype(F32)
        relu_imag = relu_ref[1, at, :].astype(F32)
        up_real = spectral[:half] * shrink_ref[0, at, :]
        up_imag = spectral[half:] * shrink_ref[1, at, :]
        hidden_real = dot(mode_real, one_real) - dot(mode_imag, one_imag) + bias_ref[0:1, :]
        hidden_imag = dot(mode_real, one_imag) + dot(mode_imag, one_real) + bias_ref[1:2, :]
        hidden_real = (relu_real * hidden_real).astype(BF16)
        hidden_imag = (relu_imag * hidden_imag).astype(BF16)
        inner_real = dot(up_real, two_real, COLS) + dot(up_imag, two_imag, COLS)
        inner_imag = dot(up_imag, two_real, COLS) - dot(up_real, two_imag, COLS)
        inner_real = (relu_real * inner_real).astype(BF16)
        inner_imag = (relu_imag * inner_imag).astype(BF16)
        grad_real = dot(inner_real, one_real, COLS) + dot(inner_imag, one_imag, COLS)
        grad_imag = dot(inner_imag, one_real, COLS) - dot(inner_real, one_imag, COLS)
        grad = jnp.concatenate([grad_real.astype(BF16), grad_imag.astype(BF16)], axis=0)
        back = [dot(back_ref[r], grad).astype(BF16) for r in range(rows)]
        back = jnp.concatenate(back, axis=1)
        if packed:
            back_out[:, g * 2 * group : (g + 1) * 2 * group, :] = back.reshape(
                owners, 2 * group, field
            )
        else:
            back_out[...] = back
        sums = (
            (second_sum, 0, dot(hidden_real, up_real, ROWS) + dot(hidden_imag, up_imag, ROWS)),
            (second_sum, 1, dot(hidden_real, up_imag, ROWS) - dot(hidden_imag, up_real, ROWS)),
            (first_sum, 0, dot(mode_real, inner_real, ROWS) + dot(mode_imag, inner_imag, ROWS)),
            (first_sum, 1, dot(mode_real, inner_imag, ROWS) - dot(mode_imag, inner_real, ROWS)),
            (bias_sum, 0, jnp.sum(inner_real.astype(F32), axis=0, keepdims=True)),
            (bias_sum, 1, jnp.sum(inner_imag.astype(F32), axis=0, keepdims=True)),
        )
        for ref, part, value in sums:
            ref[part] = value if g == 0 else ref[part] + value
    block = width // blocks
    lanes = lax.broadcasted_iota(jnp.int32, (block, width), 1)

    def diagonal(ref, part):
        value = ref[part, :block, :]
        for n in range(1, blocks):
            value = jnp.where(lanes < n * block, value, ref[part, n * block : (n + 1) * block, :])
        return value

    gathered = jnp.concatenate(
        [
            jnp.concatenate([diagonal(ref, 0), diagonal(ref, 1)], axis=1)
            for ref in (first_sum, second_sum)
        ],
        axis=0,
    ).astype(BF16)
    bias = jnp.concatenate([bias_sum[0], bias_sum[1]], axis=1).astype(BF16)
    if packed:
        per = 2 * block // owners
        start = groups * 2 * group
        tail = back_out.shape[1] - start - per
        bias = jnp.broadcast_to(bias, (tail, field))
        for j in range(owners):
            chunk = jnp.concatenate([gathered[j * per : (j + 1) * per], bias], axis=0)
            back_out[j, start:, :] = chunk
    else:
        grad_outs[0][...] = gathered
        grad_outs[1][...] = bias


def local(tokens, cotangent, first_weight, first_bias, second_weight, relu_mask, shrink_mask):
    batches, rows, blocks, flat_east = tokens.shape
    block = first_weight.shape[2]
    cells = flat_east // block
    owners = lax.axis_size("lat")
    wave_dev = WAVES // owners
    group = group_of(wave_dev)
    groups = wave_dev // group
    north = rows * owners
    width = blocks * block
    field = rows * width
    factor = 1.0 / math.sqrt(north * WAVES)

    east = jnp.asarray(east_rows(cells, WAVES, owners), BF16)
    table = north_rows(owners, rows, group)
    forward = jnp.asarray(table, BF16)
    backward = jnp.asarray(table.transpose(0, 2, 1), BF16)

    grid = jnp.stack([tokens, cotangent]).reshape(2, rows, blocks, cells, block)
    grid = grid.transpose(3, 0, 1, 2, 4).reshape(cells, 2 * field)
    waves = jnp.dot(east, grid, preferred_element_type=F32).astype(BF16)
    span = 2 * wave_dev
    waves = waves.reshape(owners, span, 2 * field)
    waves = lax.all_to_all(waves, "lat", split_axis=0, concat_axis=0, tiled=True)

    def by_mode(mask):
        mask = mask.astype(BF16).reshape(2, blocks, wave_dev, north, block)
        return mask.transpose(0, 2, 3, 1, 4).reshape(2, wave_dev * north, width)

    def diagonal(weight):
        eye = jnp.eye(blocks, dtype=weight.dtype)
        spread = weight[:, :, :, None, :] * eye[None, :, None, :, None]
        return spread.reshape(2, width, width)

    weights = jnp.concatenate([diagonal(first_weight), diagonal(second_weight)])
    bias = first_bias.reshape(2, width).astype(F32)

    packed = (2 * group) % 16 == 0 and (2 * block) % owners == 0
    per = -(-2 * block // owners)
    extra = -(-(per + 1) // 16) * 16 - per if packed else 1
    shapes = ((owners, span + per + extra, field),) if packed else (
        (owners * span, field), (2 * block, field), (1, field))
    vmem = pl.BlockSpec(memory_space=pltpu.VMEM)
    sent, *parts = pl.pallas_call(
        functools.partial(mix_kernel, (owners, groups, group, rows, blocks, width, packed)),
        out_shape=[jax.ShapeDtypeStruct(shape, BF16) for shape in shapes],
        in_specs=[vmem] * 7,
        out_specs=[vmem] * len(shapes),
        scratch_shapes=[
            pltpu.VMEM((2, width, width), F32),
            pltpu.VMEM((2, width, width), F32),
            pltpu.VMEM((2, 1, width), F32),
        ],
        name="mix",
    )(waves.reshape(owners * span, 2 * field), forward, backward, weights, bias,
      by_mode(relu_mask), by_mode(shrink_mask))
    if not packed:
        grads = jnp.pad(parts[0], ((0, owners * per - 2 * block), (0, 0)))
        biases = jnp.broadcast_to(parts[1][None], (owners, 1, field))
        sent = sent.reshape(owners, span, field)
        sent = jnp.concatenate([sent, grads.reshape(owners, per, field), biases], axis=1)
    returned = lax.all_to_all(sent, "lat", split_axis=0, concat_axis=0, tiled=True)
    back = returned[:, :span].reshape(owners * span, field)
    chunk = jnp.sum(returned[:, span:].astype(F32), axis=0) * factor
    chunk = jnp.broadcast_to(chunk.astype(BF16)[None], (owners,) + chunk.shape)
    totals = lax.all_to_all(chunk, "lat", split_axis=0, concat_axis=0, tiled=True).astype(F32)

    token = lax.dot_general(east, back, (((0,), (0,)), ((), ())), preferred_element_type=F32)
    token = (token + grid[:, field:].astype(F32)).astype(BF16)
    token = token.reshape(cells, rows, blocks, block).transpose(1, 2, 0, 3)
    token = token.reshape(batches, rows, blocks, flat_east)

    grads = totals[:, :per].reshape(owners * per, field)[: 2 * block]
    grads = grads.reshape(2, block, 2, blocks, block).transpose(0, 2, 3, 1, 4)
    bias_grad = totals[0, per].reshape(2, blocks, block)
    return (token, grads[0], bias_grad, grads[1])


def solution(mesh):
    return jax.shard_map(
        local,
        mesh=mesh,
        in_specs=(
            P(None, "lat", "ch", None),
            P(None, "lat", "ch", None),
            P(None, "ch", None, None),
            P(None, "ch", None),
            P(None, "ch", None, None),
            P(None, None, "ch", "lat", None),
            P(None, None, "ch", "lat", None),
        ),
        out_specs=(
            P(None, "lat", "ch", None),
            P(None, "ch", None, None),
            P(None, "ch", None),
            P(None, "ch", None, None),
        ),
        check_vma=False,
    )
```

time: 158 us -> 75.9 us (0.48)
  waiting for transfers between devices: 64.6 us -> 15.3 us
  between operations: 14.5 us -> 0.9 us
  matrix products: 15 us -> 2.27 us
  other arithmetic: 8.23 us -> 2.5 us
  Pallas kernels: 0 us -> 5.62 us
  starting transfers between devices: 14.6 us -> 10.8 us
  blocking collectives: 22.6 us -> 20.3 us
    psum x1 -> x0, waiting for transfers between devices: 47.6 us -> none  [local(): lax.psum((first_grad, bias_grad, second_grad), 'lat')]
    psum x1 -> x0, blocking collectives: 22.6 us -> none  [local(): lax.psum((first_grad, bias_grad, second_grad), 'lat')]
    all_to_all x0 -> x1, blocking collectives: none -> 20.3 us  [local(): lax.all_to_all(sent, 'lat', split_axis=0, concat_axis=0, tiled=True)]
    dot_general x26 -> x2, matrix products: 15 us -> 2.27 us  [the longest x1 1.69 us: local(): waves = jnp.dot(east, grid, preferred_element_type=F32).astype(BF16)]
    pallas_call x0 -> x1, Pallas kernels: none -> 5.62 us  [local(): pl.pallas_call(functools.partial(mix_kernel, (owners, groups, group, rows...]
    convert_element_type x7 -> x2, local copies, waits for them, and re-layouts: 5.82 us -> 0.91 us  [the longest x1 0.66 us: local(): bias = first_bias.reshape(2, width).astype(F32)]
    reshape x2 -> x7, local copies, waits for them, and re-layouts: 2.17 us -> 5.99 us  [the longest x2 2.24 us: by_mode(): return mask.transpose(0, 2, 3, 1, 4).reshape(2, wave_dev * north, width)]
    all_to_all x3 -> x2, starting transfers between devices: 14.6 us -> 10.8 us  [the longest x1 7.41 us: local(): lax.all_to_all(waves, 'lat', split_axis=0, concat_axis=0, tiled=True)]
  transfers between devices with their start and end apart: 4 -> 2, of which waited for: 3 -> 2; matrix products, arithmetic and copies ran while one was open for 12% -> 15% of each run, Pallas kernels for 0% -> 0%
where the time goes in v1:
time: 75.9 us; the launch traced here: 75.3 us
  blocking collectives  20.3 us (27%)
  local copies, waits for them, and re-layouts  17.7 us (23%)
  waiting for transfers between devices  15.3 us (20%)
  starting transfers between devices  10.8 us (14%)
  Pallas kernels  5.62 us (7%)
  other arithmetic  2.5 us (3%)
  matrix products  2.27 us (3%)
  between operations  0.9 us (1%)
    all_to_all x1, blocking collectives, local(): lax.all_to_all(sent, 'lat', split_axis=0, concat_axis=0, tiled=True)  20.3 us
    all_to_all x1, waiting for transfers between devices, local(): lax.all_to_all(waves, 'lat', split_axis=0, concat_axis=0, tiled=True)  11.7 us
    all_to_all x1, starting transfers between devices, local(): lax.all_to_all(waves, 'lat', split_axis=0, concat_axis=0, tiled=True)  7.41 us
    pallas_call x1, Pallas kernels, local(): pl.pallas_call(functools.partial(mix_kernel, (owners, groups, group, rows...  5.62 us
    unnamed x21, local copies, waits for them, and re-layouts  3.81 us
    all_to_all x1, waiting for transfers between devices, local(): lax.all_to_all(chunk, 'lat', split_axis=0, concat_axis=0, tiled=True)  3.59 us
    all_to_all x1, starting transfers between devices, local(): lax.all_to_all(chunk, 'lat', split_axis=0, concat_axis=0, tiled=True)  3.39 us
    another operation x2, local copies, waits for them, and re-layouts, local(): grid = jnp.stack([tokens, cotangent]).reshape(2, rows, blocks, cells, block)  2.55 us
  transfers between devices with their start and end apart: 2, of which 2 were waited for; matrix products, arithmetic and copies ran while one was open for 15% of the time, Pallas kernels for 0%

profile of v1, /device:TPU:0, one launch (start us, length us, event | category | flops | bytes accessed | tf_op | source)
XLA Modules:
  0.0 75.3 jit_solution(5724049875184628992)
XLA Ops:
  0.6 1.8 %stack.10 = bf16[1,2,2,720,96]{4,3,2,1,0:T(8,128)(2,1)S(1)} reshape(bf16[1,2,2,69120]{3,2,1,0:T(2,128)(2,1)} %param.11) | data formatting | bytes 1105920 | tf_op jit(solution)/shard_map/stack | solution.py:154
  2.5 0.7 stack.9
  3.6 0.7 copy.19
  4.7 1.7 %convolution_convert_fusion = bf16[768,512]{0,1:T(8,128)(2,1)} fusion(bf16[720,768]{0,1:T(8,128)(2,1)S(1)} %bitcast.33, bf16[512,720]{1,0:T(8,128)(2,1)S(1)} %copy-done.7), kind=kOutput, calls=%fused_computation.1 | convolution fusion | flops 566624256 | bytes 2629632 | tf_op jit(solution)/shard_map/dot_general | solution.py:156
  6.4 7.4 %all-to-all-start = ((bf16[8,64,768]{2,1,0:T(8,128)(2,1)}), bf16[8,64,768]{2,1,0:T(8,128)(2,1)S(1)}, u32[]{:S(2)}, u32[]{:S(2)}) async-start(bf16[8,64,768]{2,1,0:T(8,128)(2,1)} %bitcast.3), calls=%async_computation | async-start | bytes 1572864 | tf_op jit(solution)/shard_map/all_to_all | solution.py:159
  14.5 0.8 %mul.53 = bf16[192,192]{1,0:T(8,128)(2,1)} reshape(bf16[2,96,2,96]{3,2,1,0:T(2,128)(2,1)S(1)} %mul.52) | data formatting | bytes 147456 | tf_op jit(solution)/shard_map/mul | solution.py:167
  16.3 1.1 %reshape.70.relu_ref = bf16[2,512,192]{2,1,0:T(8,128)(2,1)} reshape(bf16[2,32,16,2,96]{4,3,2,1,0:T(2,128)(2,1)S(1)} %bitcast.36) | data formatting | bytes 786432 | tf_op jit(solution)/shard_map/reshape | solution.py:163
  17.4 1.2 %convert_element_type.52 = bf16[1,2,2,32,1536]{4,3,2,1,0:T(8,128)(2,1)S(1)} convert(s32[1,2,2,32,1536]{4,3,2,1,0:T(8,128)} %param.16) | non-fusion elementwise | flops 196608 | bytes 1179648 | tf_op jit(solution)/shard_map/convert_element_type | solution.py:162
  19.6 1.1 %reshape.72.shrink_ref = bf16[2,512,192]{2,1,0:T(8,128)(2,1)} reshape(bf16[2,32,16,2,96]{4,3,2,1,0:T(2,128)(2,1)S(1)} %bitcast.37) | data formatting | bytes 786432 | tf_op jit(solution)/shard_map/reshape | solution.py:163
  20.8 0.7 reshape.76.bias_ref
  21.4 0.8 %pad_maximum_fusion.weight_ref = bf16[4,192,192]{2,1,0:T(8,128)(2,1)} fusion(bf16[2,192,192]{2,1,0:T(8,128)(2,1)S(1)} %get-tuple-element.11, bf16[2,192,192]{2,1,0:T(8,128)(2,1)S(1)} %get-tuple-element.10), kind=kLoop, calls=%fused_computation.6 | loop fusion | flops 147456 | bytes 589824 | tf_op jit(solution)/shard_map/concatenate | solution.py:170
  22.3 11.7 %all-to-all-done = bf16[8,64,768]{2,1,0:T(8,128)(2,1)S(1)} async-done(((bf16[8,64,768]{2,1,0:T(8,128)(2,1)}), bf16[8,64,768]{2,1,0:T(8,128)(2,1)S(1)}, u32[]{:S(2)}, u32[]{:S(2)}) %all-to-all-start) | async-done | bytes 786464 | tf_op jit(solution)/shard_map/all_to_all | solution.py:159
  34.0 0.9 %copy-done = bf16[8,64,768]{2,1,0:T(8,128)(2,1)} copy-done((bf16[8,64,768]{2,1,0:T(8,128)(2,1)}, bf16[8,64,768]{2,1,0:T(8,128)(2,1)S(1)}, u32[]{:S(2)}) %copy-start) | copy-done | bytes 786456
  34.9 5.6 %mix.1 = bf16[8,96,384]{2,1,0:T(8,128)(2,1)} custom-call(bf16[512,768]{1,0:T(8,128)(2,1)} %bitcast.32, bf16[2,512,256]{2,1,0:T(8,128)(2,1)} %constant.11.clone.table_ref, bf16[2,256,512]{2,1,0:T(8,128)(2,1)} %constant.12.clone.back_ref, bf16[4,192,192]{2,1,0:T(8,128)(2,1)} %pad_maximum_fusion.weight_ref, f32[2,192]{1,0:T(2,128)} %reshape.76.bias_ref, ...), custom_call_target="tpu_custom_call" | custom-call | tf_op jit(solution)/shard_map/mix/pallas_call | solution.py:179
  40.5 20.3 %all_to_all.15 = bf16[8,96,384]{2,1,0:T(8,128)(2,1)S(1)} all-to-all(bf16[8,96,384]{2,1,0:T(8,128)(2,1)} %mix.1), channel_id=1, replica_groups=mesh['lat'=8,'ch'=4] {'lat'}, dimensions={0} | all-to-all | bytes 1179648 | tf_op jit(solution)/shard_map/all_to_all | solution.py:197
  60.8 0.7 broadcast_in_dim.2
  61.5 3.4 %all-to-all-start.2 = ((bf16[8,32,384]{2,1,0:T(8,128)(2,1)}), bf16[8,32,384]{2,1,0:T(8,128)(2,1)S(1)}, u32[]{:S(2)}, u32[]{:S(2)}) async-start(bf16[8,32,384]{2,1,0:T(8,128)(2,1)} %broadcast_in_dim.2), calls=%async_computation.2 | async-start | bytes 393216 | tf_op jit(solution)/shard_map/all_to_all | solution.py:201
  65.3 0.8 %copy-done.8 = bf16[512,720]{1,0:T(8,128)(2,1)S(1)} copy-done((bf16[512,720]{1,0:T(8,128)(2,1)S(1)}, bf16[512,720]{1,0:T(8,128)(2,1)}, u32[]{:S(2)}) %copy-start.8) | copy-done | bytes 737304
  66.1 0.6 fusion
  67.3 1.8 %reshape.75 = bf16[1,2,2,69120]{3,2,1,0:T(2,128)(2,1)} reshape(bf16[2,2,720,96]{3,2,1,0:T(8,128)(2,1)S(1)} %copy.24) | data formatting | bytes 1105920 | tf_op jit(solution)/shard_map/reshape | solution.py:206
  69.0 3.6 %all-to-all-done.2 = bf16[8,32,384]{2,1,0:T(8,128)(2,1)S(1)} async-done(((bf16[8,32,384]{2,1,0:T(8,128)(2,1)}), bf16[8,32,384]{2,1,0:T(8,128)(2,1)S(1)}, u32[]{:S(2)}, u32[]{:S(2)}) %all-to-all-start.2) | async-done | bytes 196640 | tf_op jit(solution)/shard_map/all_to_all | solution.py:201
  73.2 0.7 copy.25
  73.9 0.7 copy.26
  74.7 0.7 reshape_squeeze.3
  (41 shorter events, 5.1 us)
Async XLA Ops:
  0.6 1.8 %copy-start.2 = (bf16[1,2,2,69120]{3,2,1,0:T(2,128)(2,1)S(1)}, bf16[1,2,2,69120]{3,2,1,0:T(2,128)(2,1)}, u32[]{:S(2)}) copy-start(bf16[1,2,2,69120]{3,2,1,0:T(2,128)(2,1)} %param.10) | copy-start | bytes 1658884
  3.6 1.1 %copy-start.7 = (bf16[512,720]{1,0:T(8,128)(2,1)S(1)}, bf16[512,720]{1,0:T(8,128)(2,1)}, u32[]{:S(2)}) copy-start(bf16[512,720]{1,0:T(8,128)(2,1)} %constant.10.clone) | copy-start | bytes 2211844
  6.4 7.4 %copy-start.4 = (bf16[2,2,96,96]{3,2,1,0:T(8,128)(2,1)S(1)}, bf16[2,2,96,96]{3,2,1,0:T(8,128)(2,1)}, u32[]{:S(2)}) copy-start(bf16[2,2,96,96]{3,2,1,0:T(8,128)(2,1)} %param.12) | copy-start | bytes 221188
  6.4 7.7 %copy-start.5 = (bf16[2,2,96,96]{3,2,1,0:T(8,128)(2,1)S(1)}, bf16[2,2,96,96]{3,2,1,0:T(8,128)(2,1)}, u32[]{:S(2)}) copy-start(bf16[2,2,96,96]{3,2,1,0:T(8,128)(2,1)} %param.14) | copy-start | bytes 221188
  6.4 27.6 %all-to-all-start = ((bf16[8,64,768]{2,1,0:T(8,128)(2,1)}), bf16[8,64,768]{2,1,0:T(8,128)(2,1)S(1)}, u32[]{:S(2)}, u32[]{:S(2)}) async-start(bf16[8,64,768]{2,1,0:T(8,128)(2,1)} %bitcast.3), calls=%async_computation | async-start | bytes 1572864 | tf_op jit(solution)/shard_map/all_to_all | solution.py:159
  13.8 1.4 %copy-start.1 = (s32[1,2,2,32,1536]{4,3,2,1,0:T(8,128)S(1)}, s32[1,2,2,32,1536]{4,3,2,1,0:T(8,128)}, u32[]{:S(2)}) copy-start(s32[1,2,2,32,1536]{4,3,2,1,0:T(8,128)} %param.15) | copy-start | bytes 2359300
  19.1 1.7 %copy-start.6 = (bf16[2,2,96]{2,1,0:T(2,128)(2,1)S(1)}, bf16[2,2,96]{2,1,0:T(2,128)(2,1)}, u32[]{:S(2)}) copy-start(bf16[2,2,96]{2,1,0:T(2,128)(2,1)} %param.13) | copy-start | bytes 2308
  19.1 2.4 %copy-start.3 = (bf16[192,192]{1,0:T(8,128)(2,1)S(1)}, bf16[192,192]{1,0:T(8,128)(2,1)}, u32[]{:S(2)}) copy-start(bf16[192,192]{1,0:T(8,128)(2,1)} %mul.53) | copy-start | bytes 221188
  34.0 0.9 %copy-start = (bf16[8,64,768]{2,1,0:T(8,128)(2,1)}, bf16[8,64,768]{2,1,0:T(8,128)(2,1)S(1)}, u32[]{:S(2)}) copy-start(bf16[8,64,768]{2,1,0:T(8,128)(2,1)S(1)} %all-to-all-done) | copy-start | bytes 2359300
  61.5 11.1 %all-to-all-start.2 = ((bf16[8,32,384]{2,1,0:T(8,128)(2,1)}), bf16[8,32,384]{2,1,0:T(8,128)(2,1)S(1)}, u32[]{:S(2)}, u32[]{:S(2)}) async-start(bf16[8,32,384]{2,1,0:T(8,128)(2,1)} %broadcast_in_dim.2), calls=%async_computation.2 | async-start | bytes 393216 | tf_op jit(solution)/shard_map/all_to_all | solution.py:201
  64.9 1.1 %copy-start.8 = (bf16[512,720]{1,0:T(8,128)(2,1)S(1)}, bf16[512,720]{1,0:T(8,128)(2,1)}, u32[]{:S(2)}) copy-start(bf16[512,720]{1,0:T(8,128)(2,1)} %constant.10.clone) | copy-start | bytes 2211844
